TPU v7x, 32 devices: a whole 2x2x4 slice. The times are simulated.
32 devices in a mesh: groups: 2 (over y), expert: 4 (over z), dp: 2 (over x), tile: 2 (over core).
Axes of the slice: x: 2, y: 2, z: 4, core: 2. Of those that a mesh axis runs over, the one named last changes fastest.
Arguments:
- features: bfloat16 [256, 1024], P(('groups', 'expert', 'dp', 'tile')), parts along dimension 0, may hold values from -6 to 6
- cross_weight: bfloat16 [1024, 1024], P(None, ('dp', 'tile')), may hold values from -0.1875 to 0.1875
- cross_bias: float32 [1024], replicated, may hold values from -1 to 1
- gate_weight: bfloat16 [1024, 36], replicated, may hold values from -24 to 24
- unit_experts: int32 [6, 6], replicated, may hold values from 0 to 15, all different within a row
- up_weight: bfloat16 [1024, 65536], P(None, ('expert', 'dp')), may hold values from -0.1875 to 0.1875
- up_bias: float32 [65536], P(('expert', 'dp')), may hold values from -3 to 3
- down_weight: bfloat16 [65536, 512], P(('expert', 'dp')), may hold values from -0.09375 to 0.09375
- down_bias: float32 [16, 512], replicated, may hold values from -3 to 3
- task_counts: int32 [32, 6], P(('groups', 'expert', 'dp', 'tile')), parts along dimension 0, may hold values from 1 to 8, as said below
- tower_in: bfloat16 [6, 512, 2048], P(None, None, ('dp', 'tile')), may hold values from -0.25 to 0.25
- tower_in_bias: float32 [6, 2048], P(None, ('dp', 'tile')), may hold values from -3 to 3
- tower_out: bfloat16 [6, 2048, 512], P(None, ('dp', 'tile')), may hold values from -0.125 to 0.125
- tower_out_bias: float32 [6, 512], replicated, may hold values from -3 to 3
Outputs:
- task_states: bfloat16 [256, 6, 512], P(('groups', 'expert', 'dp', 'tile')), parts along dimension 0
There are 2 independent parts, one for each index of `groups`. A program takes and returns all parts, laid end to end along the dimension named above; an argument that names none is the same for every part. Nothing has to cross between parts.
Inputs may be any that keep to these rules, and one draw needn't show every extreme that they name: `task_counts`: every task reaches a count of 8 on some row shard; which one is drawn from the seed.
All inputs are finite; a program needn't handle non-finite values.
Results may differ from a plain program's by a relative error of at most 0.0095.
Values may be sent and summed in bfloat16 or wider, within the bound.
A program may use at most 64 MiB of HBM per device.

v0:
```python
import jax
import jax.numpy as jnp
from jax import lax
from jax.sharding import PartitionSpec as P

EXPERT_FF = 4096


def body(
    features,
    cross_weight,
    cross_bias,
    gate_weight,
    unit_experts,
    up_weight,
    up_bias,
    down_weight,
    down_bias,
    task_counts,
    tower_in,
    tower_in_bias,
    tower_out,
    tower_out_bias,
):
    rows_own = features.shape[0]
    task_count = unit_experts.shape[0]
    unit_width = unit_experts.shape[1]
    out_width = down_weight.shape[1]
    column_base = features.astype(jnp.float32)
    scaled = (
        jnp.dot(
            features,
            lax.all_gather(cross_weight, ("dp", "tile"), axis=1, tiled=True),
            preferred_element_type=jnp.float32,
        )
        + cross_bias
    )
    crossed = (column_base * scaled + column_base).astype(jnp.bfloat16)
    logits = jnp.dot(features, gate_weight, preferred_element_type=jnp.float32)
    gate_probs = jax.nn.softmax(logits.reshape(rows_own, task_count, unit_width), axis=-1)
    hid_dev = up_weight.shape[1]
    pieces = max(1, hid_dev // EXPERT_FF)
    piece_width = hid_dev // pieces
    down_split = down_weight.reshape(pieces, piece_width, out_width)
    row_piece = lax.all_gather(crossed, ("expert", "dp"), axis=0, tiled=True)
    hidden = jnp.dot(row_piece, up_weight, preferred_element_type=jnp.float32) + up_bias
    hidden = (
        jax.nn.relu(hidden).astype(jnp.bfloat16).reshape(row_piece.shape[0], pieces, piece_width)
    )
    partial_value = jnp.einsum(
        "rpw,pwo->rpo", hidden, down_split, preferred_element_type=jnp.float32
    )
    expert_size = lax.axis_size("expert")
    data_size = lax.axis_size("dp")
    sources = expert_size * data_size
    blocks = partial_value.reshape(sources, rows_own, pieces, out_width)
    returned = lax.all_to_all(blocks, ("expert", "dp"), split_axis=0, concat_axis=0, tiled=True)
    per_expert = EXPERT_FF // piece_width
    ordered = jnp.moveaxis(returned, 2, 1).reshape(
        sources * pieces // per_expert, per_expert, rows_own, out_width
    )
    expert_out = jnp.sum(ordered, axis=1) + down_bias[:, None, :]
    onehot = (
        unit_experts[:, :, None] == jnp.arange(expert_out.shape[0], dtype=jnp.int32)[None, None, :]
    ).astype(jnp.float32)
    mix_weights = jnp.einsum("rtk,tke->rte", gate_probs, onehot)
    mixed_rows = jnp.einsum("rte,ero->rto", mix_weights, expert_out).astype(jnp.bfloat16)
    everyone = lax.all_gather(mixed_rows, ("dp", "tile"), axis=0, tiled=True)
    hidden = jnp.einsum("rto,toh->rth", everyone, tower_in, preferred_element_type=jnp.float32)
    hidden = jax.nn.relu(hidden + tower_in_bias[None, :, :]).astype(jnp.bfloat16)
    summed = lax.psum_scatter(
        jnp.einsum("rth,tho->rto", hidden, tower_out, preferred_element_type=jnp.float32),
        ("dp", "tile"),
        scatter_dimension=0,
        tiled=True,
    )
    tower_result = summed + tower_out_bias[None, :, :]
    position = jnp.arange(rows_own, dtype=jnp.int32)[:, None]
    active = position < task_counts
    return jnp.where(active[:, :, None], tower_result, 0.0).astype(jnp.bfloat16)


def solution(mesh):
    return jax.shard_map(
        body,
        mesh=mesh,
        in_specs=(
            P(("groups", "expert", "dp", "tile"), None),
            P(None, ("dp", "tile")),
            P(),
            P(),
            P(),
            P(None, ("expert", "dp")),
            P(("expert", "dp")),
            P(("expert", "dp"), None),
            P(),
            P(("groups", "expert", "dp", "tile"), None),
            P(None, None, ("dp", "tile")),
            P(None, ("dp", "tile")),
            P(None, ("dp", "tile"), None),
            P(),
        ),
        out_specs=P(("groups", "expert", "dp", "tile"), None, None),
        check_vma=False,
    )
```

profile of v0, /device:TPU:0, one launch (start us, length us, event | category | flops | bytes accessed | tf_op | source)
XLA Modules:
  0.0 128.5 jit_solution(7548105126115898000)
XLA Ops:
  6.5 0.0 copy-start
  6.5 0.0 all-gather.2.cloned.1.call-start
  6.5 0.7 all-gather.2.cloned.1.call-update
  7.3 1.3 fusion.21
  8.5 0.1 reshape.43
  8.6 25.9 %all-gather.2.cloned.1.call-done = bf16[1024,1024]{1,0:T(8,128)(2,1)} async-done(((bf16[1024,256]{1,0:T(8,128)(2,1)}), bf16[1024,1024]{1,0:T(8,128)(2,1)}) %all-gather.2.cloned.1.call-update) | async-done | bytes 2097168 | tf_op jit(solution)/shard_map/all_gather | solution.py:33
  34.5 0.0 slice-start
  34.5 2.1 %fusion.10 = bf16[8,1024]{1,0:T(8,128)(2,1)S(1)} fusion(bf16[8,1024]{1,0:T(8,128)(2,1)} %param.14, bf16[1024,1024]{1,0:T(8,128)(2,1)} %all-gather.2.cloned.1.call-done, f32[1024]{0:T(1024)} %param.16), kind=kOutput, calls=%fused_computation.16 | convolution fusion | flops 16818176 | bytes 2134016 | tf_op jit(solution)/shard_map/dot_general | solution.py:31
  36.6 30.6 %all_gather.10 = bf16[64,1024]{1,0:T(8,128)(2,1)S(1)} all-gather(bf16[8,1024]{1,0:T(8,128)(2,1)S(1)} %fusion.10), channel_id=1, replica_groups=mesh['groups'=2,'expert'=4,'dp'=2,'tile'=2] {'expert','dp'}, dimensions={0}, use_global_device_ids=true | all-gather | bytes 147456 | tf_op jit(solution)/shard_map/all_gather | solution.py:45
  67.2 0.0 slice-start.1
  67.2 8.9 %fusion.2 = bf16[64,8192]{1,0:T(8,128)(2,1)S(1)} fusion(bf16[64,1024]{1,0:T(8,128)(2,1)S(1)} %all_gather.10, bf16[1024,8192]{1,0:T(8,128)(2,1)} %param.19, f32[8192]{0:T(1024)} %param.20), kind=kOutput, calls=%fused_computation.3 | convolution fusion | flops 1075314688 | bytes 17989632 | tf_op jit(solution)/shard_map/dot_general | solution.py:46
  76.1 0.0 slice-done
  76.1 0.0 slice-done.1
  76.1 0.0 copy-start.4
  76.2 0.0 copy-start.1
  76.2 0.0 copy-start.2
  76.2 1.6 %convolution_bitcast_fusion.1 = f32[8,8,2,512]{3,1,0,2:T(8,128)S(1)} fusion(bf16[2,4096,512]{2,1,0:T(8,128)(2,1)S(1)} %bitcast.35, bf16[8,2,8,4096]{3,2,1,0:T(8,128)(2,1)S(1)} %bitcast.36), kind=kOutput, calls=%fused_computation.8 | convolution fusion | flops 536870912 | bytes 9699328 | tf_op jit(solution)/shard_map/rpw,pwo->rpo/dot_general | solution.py:50
  77.7 0.7 copy.20
  78.5 4.5 %all-to-all-start = ((f32[8,8,2,512]{3,1,2,0:T(8,128)}), f32[8,8,2,512]{3,1,2,0:T(8,128)S(1)}, u32[]{:S(2)}, u32[]{:S(2)}) async-start(f32[8,8,2,512]{3,1,2,0:T(8,128)} %copy.20), calls=%async_computation | async-start | bytes 524288 | tf_op jit(solution)/shard_map/all_to_all | solution.py:57
  83.0 0.0 reduce-scatter.2.cloned.1.call-start
  83.1 1.3 %fusion.20 = (f32[8,6]{1,0:T(8,128)S(1)}, f32[8,6,6]{2,1,0:T(8,128)S(1)}) fusion(f32[8,6,6]{2,1,0:T(8,128)S(1)} %reshape.43), kind=kOutput, calls=%fused_computation.32 | output fusion | flops 581 | bytes 2496 | tf_op jit(solution)/shard_map/sub | solution.py:40
  84.4 0.1 broadcast_divide_fusion
  84.5 0.0 copy-done.4
  84.5 0.2 convolution_bitcast_fusion.2
  84.7 6.5 %all-to-all-done = f32[8,8,2,512]{3,1,2,0:T(8,128)S(1)} async-done(((f32[8,8,2,512]{3,1,2,0:T(8,128)}), f32[8,8,2,512]{3,1,2,0:T(8,128)S(1)}, u32[]{:S(2)}, u32[]{:S(2)}) %all-to-all-start) | async-done | bytes 262176 | tf_op jit(solution)/shard_map/all_to_all | solution.py:57
  91.2 0.0 copy-done.1
  91.3 0.2 convolution_convert_fusion
  91.5 5.6 %all_gather.11 = bf16[32,6,512]{2,0,1:T(8,128)(2,1)S(1)} all-gather(bf16[8,6,512]{2,0,1:T(8,128)(2,1)S(1)} %copy.23), channel_id=1, replica_groups=mesh['groups'=2,'expert'=4,'dp'=2,'tile'=2] {'dp','tile'}, dimensions={0}, use_global_device_ids=true | all-gather | bytes 245760 | tf_op jit(solution)/shard_map/all_gather | solution.py:68
  97.1 0.0 copy-done
  97.1 0.0 copy-done.2
  97.1 0.0 copy-start.5
  97.1 0.0 copy-start.3
  97.1 3.8 %convolution_bitcast_fusion = f32[32,6,512]{2,0,1:T(8,128)} fusion(bf16[6,512,512]{2,1,0:T(8,128)(2,1)S(1)} %copy-done, bf16[32,6,512]{2,0,1:T(8,128)(2,1)S(1)} %all_gather.11, bf16[6,512,512]{2,1,0:T(8,128)(2,1)} %param.24, f32[6,512]{1,0:T(8,128)S(1)} %copy-done.2), kind=kOutput, calls=%fused_computation.4 | convolution fusion | flops 201621504 | bytes 6893568 | tf_op jit(solution)/shard_map/rth,tho->rto/dot_general | solution.py:72
  100.8 0.0 reduce-scatter.2.cloned.1.call-update
  100.9 0.0 copy-done.5
  100.9 0.1 iota_compare_fusion.2
  101.0 19.2 %reduce-scatter.2.cloned.1.call-done = f32[8,6,512]{2,0,1:T(8,128)} async-done(((f32[32,6,512]{2,0,1:T(8,128)}), f32[8,6,512]{2,0,1:T(8,128)}) %reduce-scatter.2.cloned.1.call-update) | async-done | bytes 98320 | tf_op jit(solution)/shard_map/reduce_scatter | solution.py:71
  120.1 0.0 copy-done.3
  120.1 1.6 %select_convert_fusion = bf16[8,6,512]{2,0,1:T(8,128)(2,1)} fusion(f32[8,6,512]{2,0,1:T(8,128)} %reduce-scatter.2.cloned.1.call-done, f32[6,512]{1,0:T(8,128)S(1)} %copy-done.3, pred[8,6]{0,1:T(8,128)(4,1)S(1)} %iota_compare_fusion.2), kind=kLoop, calls=%fused_computation.24 | loop fusion | flops 73728 | bytes 159792 | tf_op jit(solution)/shard_map/convert_element_type | solution.py:80
  (3 shorter events, 0.1 us)
Async XLA Ops:
  6.5 90.5 %copy-start = (bf16[6,512,512]{2,1,0:T(8,128)(2,1)S(1)}, bf16[6,512,512]{2,1,0:T(8,128)(2,1)}, u32[]{:S(2)}) copy-start(bf16[6,512,512]{2,1,0:T(8,128)(2,1)} %param.26) | copy-start | bytes 9437188
  6.5 27.9 %all-gather.2.cloned.1.call-start = ((), (), s32[]{:S(2)}) async-start(), calls=%async_computation.2 | async-start | bytes 2621440 | tf_op jit(solution)/shard_map/all_gather | solution.py:33
  34.5 41.7 %slice-start = ((s8[8388608]{0:T(1024)(128)(4,1)}), s8[4194304]{0:T(1024)(128)(4,1)S(1)}, s32[]{:S(2)}) async-start(s8[8388608]{0:T(1024)(128)(4,1)} %bitcast.33), calls=%async_computation.4 | async-start | bytes 8388608
  67.2 9.0 %slice-start.1 = ((s8[8388608]{0:T(1024)(128)(4,1)}), s8[4194304]{0:T(1024)(128)(4,1)S(1)}, s32[]{:S(2)}) async-start(s8[8388608]{0:T(1024)(128)(4,1)} %bitcast.33), calls=%async_computation.5 | async-start | bytes 8388608
  76.1 8.3 %copy-start.4 = (s32[6,6]{1,0:T(8,128)S(1)}, s32[6,6]{1,0:T(8,128)}, u32[]{:S(2)}) copy-start(s32[6,6]{1,0:T(8,128)} %param.18) | copy-start | bytes 436
  76.2 15.1 %copy-start.1 = (f32[16,512]{1,0:T(8,128)S(1)}, f32[16,512]{1,0:T(8,128)}, u32[]{:S(2)}) copy-start(f32[16,512]{1,0:T(8,128)} %param.22) | copy-start | bytes 98308
  76.2 20.9 %copy-start.2 = (f32[6,512]{1,0:T(8,128)S(1)}, f32[6,512]{1,0:T(8,128)}, u32[]{:S(2)}) copy-start(f32[6,512]{1,0:T(8,128)} %param.25) | copy-start | bytes 36868
  78.5 12.8 %all-to-all-start = ((f32[8,8,2,512]{3,1,2,0:T(8,128)}), f32[8,8,2,512]{3,1,2,0:T(8,128)S(1)}, u32[]{:S(2)}, u32[]{:S(2)}) async-start(f32[8,8,2,512]{3,1,2,0:T(8,128)} %copy.20), calls=%async_computation | async-start | bytes 524288 | tf_op jit(solution)/shard_map/all_to_all | solution.py:57
  83.0 37.1 %reduce-scatter.2.cloned.1.call-start = ((), (), s32[]{:S(2)}) async-start(), calls=%async_computation.3 | async-start | bytes 491520 | tf_op jit(solution)/shard_map/reduce_scatter | solution.py:71
  97.1 3.8 %copy-start.5 = (s32[1,6]{1,0:T(1,128)S(1)}, s32[1,6]{1,0:T(1,128)}, u32[]{:S(2)}) copy-start(s32[1,6]{1,0:T(1,128)} %param.23) | copy-start | bytes 76
  97.1 23.0 %copy-start.3 = (f32[6,512]{1,0:T(8,128)S(1)}, f32[6,512]{1,0:T(8,128)}, u32[]{:S(2)}) copy-start(f32[6,512]{1,0:T(8,128)} %param.27) | copy-start | bytes 36868
Sparse Core Ops, SparseCore 0:
  8.9 25.5 all-gather.1
  101.0 19.0 reduce-scatter.1
where the time goes:
time: 129 us
  waiting for transfers between devices  52.3 us (41%)
  blocking collectives  36.2 us (28%)
  matrix products  18 us (14%)
  between operations  13.5 us (10%)
  starting transfers between devices  4.57 us (4%)
  other arithmetic  3.11 us (2%)
    all_gather x1, blocking collectives, body(): row_piece = lax.all_gather(crossed, ('expert', 'dp'), axis=0, tiled=True)  30.6 us
    all_gather x1, waiting for transfers between devices, body(): lax.all_gather(cross_weight, ('dp', 'tile'), axis=1, tiled=True)  25.9 us
    reduce_scatter x1, waiting for transfers between devices, body(): lax.psum_scatter(jnp.einsum('rth,tho->rto', hidden, tower_out, preferred_...  19.2 us
    dot_general x1, matrix products, body(): jnp.dot(row_piece, up_weight, preferred_element_type=jnp.float32) + up_bias  8.94 us
    all_to_all x1, waiting for transfers between devices, body(): lax.all_to_all(blocks, ('expert', 'dp'), split_axis=0, concat_axis=0, til...  6.55 us
    all_gather x1, blocking collectives, body(): everyone = lax.all_gather(mixed_rows, ('dp', 'tile'), axis=0, tiled=True)  5.6 us
    all_to_all x1, starting transfers between devices, body(): lax.all_to_all(blocks, ('expert', 'dp'), split_axis=0, concat_axis=0, til...  4.53 us
    dot_general x1, matrix products, body(): jnp.einsum('rth,tho->rto', hidden, tower_out, preferred_element_type=jnp....  3.77 us
  transfers between devices with their start and end apart: 3, of which 3 were waited for; matrix products, arithmetic and copies ran while one was open for 2% of the time, Pallas kernels for 0%

commit v1 on v0

--- a/solution.py
+++ b/solution.py
@@ -42,7 +42,16 @@
     pieces = max(1, hid_dev // EXPERT_FF)
     piece_width = hid_dev // pieces
     down_split = down_weight.reshape(pieces, piece_width, out_width)
-    row_piece = lax.all_gather(crossed, ("expert", "dp"), axis=0, tiled=True)
+    ways = lax.axis_size(("expert", "dp"))
+    parts = [crossed]
+    for far in range(1, ways):
+        parts.append(
+            lax.ppermute(
+                parts[far - 1], ("expert", "dp"), [(d, (d - 1) % ways) for d in range(ways)]
+            )
+        )
+    line = jnp.concatenate(parts, axis=0)
+    row_piece = jnp.roll(line, lax.axis_index(("expert", "dp")) * crossed.shape[0], axis=0)
     hidden = jnp.dot(row_piece, up_weight, preferred_element_type=jnp.float32) + up_bias
     hidden = (
         jax.nn.relu(hidden).astype(jnp.bfloat16).reshape(row_piece.shape[0], pieces, piece_width)

time: 129 us -> 144 us (1.12)
  starting transfers between devices: 4.57 us -> 39.7 us
  blocking collectives: 36.2 us -> 5.6 us
  waiting for transfers between devices: 52.3 us -> 62.6 us
    ppermute x0 -> x7, starting transfers between devices: none -> 33.4 us  [body(): lax.ppermute(parts[far - 1], ('expert', 'dp'), [(d, (d - 1) % ways) for d...]
    all_gather x1 -> x0, blocking collectives: 30.6 us -> none  [body(): row_piece = lax.all_gather(crossed, ('expert', 'dp'), axis=0, tiled=True)]
    ppermute x0 -> x7, waiting for transfers between devices: none -> 8.98 us  [body(): lax.ppermute(parts[far - 1], ('expert', 'dp'), [(d, (d - 1) % ways) for d...]
    all_to_all x1, starting transfers between devices: 4.53 us -> 6.27 us  [body(): lax.all_to_all(blocks, ('expert', 'dp'), split_axis=0, concat_axis=0, til...]
  transfers between devices with their start and end apart: 3 -> 10, of which waited for: 3 -> 10; matrix products, arithmetic and copies ran while one was open for 2% -> 2% of each run, Pallas kernels for 0% -> 0%
where the time goes in v1:
time: 144 us; the launch traced here: 143 us
  waiting for transfers between devices  62.6 us (43%)
  starting transfers between devices  39.7 us (28%)
  matrix products  17.6 us (12%)
  between operations  13.6 us (9%)
  blocking collectives  5.6 us (4%)
  other arithmetic  3.11 us (2%)
    ppermute x7, starting transfers between devices, body(): lax.ppermute(parts[far - 1], ('expert', 'dp'), [(d, (d - 1) % ways) for d...  33.4 us
    all_gather x1, waiting for transfers between devices, body(): lax.all_gather(cross_weight, ('dp', 'tile'), axis=1, tiled=True)  27.2 us
    reduce_scatter x1, waiting for transfers between devices, body(): lax.psum_scatter(jnp.einsum('rth,tho->rto', hidden, tower_out, preferred_...  19.2 us
    ppermute x7, waiting for transfers between devices, body(): lax.ppermute(parts[far - 1], ('expert', 'dp'), [(d, (d - 1) % ways) for d...  8.98 us
    dot_general x1, matrix products, body(): jnp.dot(row_piece, up_weight, preferred_element_type=jnp.float32) + up_bias  8.95 us
    all_to_all x1, waiting for transfers between devices, body(): lax.all_to_all(blocks, ('expert', 'dp'), split_axis=0, concat_axis=0, til...  6.55 us
    all_to_all x1, starting transfers between devices, body(): lax.all_to_all(blocks, ('expert', 'dp'), split_axis=0, concat_axis=0, til...  6.27 us
    all_gather x1, blocking collectives, body(): everyone = lax.all_gather(mixed_rows, ('dp', 'tile'), axis=0, tiled=True)  5.6 us
  transfers between devices with their start and end apart: 10, of which 10 were waited for; matrix products, arithmetic and copies ran while one was open for 2% of the time, Pallas kernels for 0%

profile of v1, /device:TPU:0, one launch (start us, length us, event | category | flops | bytes accessed | tf_op | source)
XLA Modules:
  0.0 143.2 jit_solution(8521217423959845287)
XLA Ops:
  6.5 0.0 copy-start
  6.5 0.0 all-gather.2.cloned.1.call-start
  6.5 0.7 all-gather.2.cloned.1.call-update
  7.3 27.2 %all-gather.2.cloned.1.call-done = bf16[1024,1024]{1,0:T(8,128)(2,1)} async-done(((bf16[1024,256]{1,0:T(8,128)(2,1)}), bf16[1024,1024]{1,0:T(8,128)(2,1)}) %all-gather.2.cloned.1.call-update) | async-done | bytes 2097168 | tf_op jit(solution)/shard_map/all_gather | solution.py:33
  34.5 2.0 %constant_dynamic-update-slice_fusion.15 = (bf16[128,1024]{1,0:T(8,128)(2,1)S(1)}, bf16[8,1024]{1,0:T(8,128)(2,1)S(1)}) fusion(f32[1024]{0:T(1024)} %param.16, bf16[8,1024]{1,0:T(8,128)(2,1)} %param.14, bf16[1024,1024]{1,0:T(8,128)(2,1)} %all-gather.2.cloned.1.call-done), kind=kOutput, calls=%fused_computation.41 | convolution fusion | flops 16818176 | bytes 2166784 | tf_op jit(solution)/shard_map/dot_general | solution.py:31
  36.4 3.3 %collective-permute-start = (bf16[8,1024]{1,0:T(8,128)(2,1)S(1)}, bf16[8,1024]{1,0:T(8,128)(2,1)S(1)}, u32[]{:S(2)}, u32[]{:S(2)}) collective-permute-start(bf16[8,1024]{1,0:T(8,128)(2,1)S(1)} %get-tuple-element.6), channel_id=1, source_target_pairs={{0,14},{2,0},{4,2},{6,4},{8,6},{10,8},{12,10},{14,12},{1,15},{3,1}... | collective-permute-start | bytes 49160 | tf_op jit(solution)/shard_map/ppermute | solution.py:49
  39.8 1.0 fusion.23
  40.8 0.1 reshape.43
  40.9 0.3 collective-permute-done
  41.2 5.0 %collective-permute-start.1 = (bf16[8,1024]{1,0:T(8,128)(2,1)S(1)}, bf16[8,1024]{1,0:T(8,128)(2,1)S(1)}, u32[]{:S(2)}, u32[]{:S(2)}) collective-permute-start(bf16[8,1024]{1,0:T(8,128)(2,1)S(1)} %collective-permute-done), channel_id=1, source_target_pairs={{0,14},{2,0},{4,2},{6,4},{8,6},{10,8},{12,10},{14,12},{1,15},{3,1}... | collective-permute-start | bytes 49160 | tf_op jit(solution)/shard_map/ppermute | solution.py:49
  46.2 1.4 %collective-permute-done.1 = bf16[8,1024]{1,0:T(8,128)(2,1)S(1)} collective-permute-done((bf16[8,1024]{1,0:T(8,128)(2,1)S(1)}, bf16[8,1024]{1,0:T(8,128)(2,1)S(1)}, u32[]{:S(2)}, u32[]{:S(2)}) %collective-permute-start.1) | collective-permute-done | bytes 16416 | tf_op jit(solution)/shard_map/ppermute | solution.py:49
  47.6 5.0 %collective-permute-start.2 = (bf16[8,1024]{1,0:T(8,128)(2,1)S(1)}, bf16[8,1024]{1,0:T(8,128)(2,1)S(1)}, u32[]{:S(2)}, u32[]{:S(2)}) collective-permute-start(bf16[8,1024]{1,0:T(8,128)(2,1)S(1)} %collective-permute-done.1), channel_id=1, source_target_pairs={{0,14},{2,0},{4,2},{6,4},{8,6},{10,8},{12,10},{14,12},{1,15},{3,1}... | collective-permute-start | bytes 49160 | tf_op jit(solution)/shard_map/ppermute | solution.py:49
  52.6 1.4 %collective-permute-done.2 = bf16[8,1024]{1,0:T(8,128)(2,1)S(1)} collective-permute-done((bf16[8,1024]{1,0:T(8,128)(2,1)S(1)}, bf16[8,1024]{1,0:T(8,128)(2,1)S(1)}, u32[]{:S(2)}, u32[]{:S(2)}) %collective-permute-start.2) | collective-permute-done | bytes 16416 | tf_op jit(solution)/shard_map/ppermute | solution.py:49
  54.1 5.0 %collective-permute-start.3 = (bf16[8,1024]{1,0:T(8,128)(2,1)S(1)}, bf16[8,1024]{1,0:T(8,128)(2,1)S(1)}, u32[]{:S(2)}, u32[]{:S(2)}) collective-permute-start(bf16[8,1024]{1,0:T(8,128)(2,1)S(1)} %collective-permute-done.2), channel_id=1, source_target_pairs={{0,14},{2,0},{4,2},{6,4},{8,6},{10,8},{12,10},{14,12},{1,15},{3,1}... | collective-permute-start | bytes 49160 | tf_op jit(solution)/shard_map/ppermute | solution.py:49
  59.1 1.4 %collective-permute-done.3 = bf16[8,1024]{1,0:T(8,128)(2,1)S(1)} collective-permute-done((bf16[8,1024]{1,0:T(8,128)(2,1)S(1)}, bf16[8,1024]{1,0:T(8,128)(2,1)S(1)}, u32[]{:S(2)}, u32[]{:S(2)}) %collective-permute-start.3) | collective-permute-done | bytes 16416 | tf_op jit(solution)/shard_map/ppermute | solution.py:49
  60.5 5.0 %collective-permute-start.4 = (bf16[8,1024]{1,0:T(8,128)(2,1)S(1)}, bf16[8,1024]{1,0:T(8,128)(2,1)S(1)}, u32[]{:S(2)}, u32[]{:S(2)}) collective-permute-start(bf16[8,1024]{1,0:T(8,128)(2,1)S(1)} %collective-permute-done.3), channel_id=1, source_target_pairs={{0,14},{2,0},{4,2},{6,4},{8,6},{10,8},{12,10},{14,12},{1,15},{3,1}... | collective-permute-start | bytes 49160 | tf_op jit(solution)/shard_map/ppermute | solution.py:49
  65.5 1.4 %collective-permute-done.4 = bf16[8,1024]{1,0:T(8,128)(2,1)S(1)} collective-permute-done((bf16[8,1024]{1,0:T(8,128)(2,1)S(1)}, bf16[8,1024]{1,0:T(8,128)(2,1)S(1)}, u32[]{:S(2)}, u32[]{:S(2)}) %collective-permute-start.4) | collective-permute-done | bytes 16416 | tf_op jit(solution)/shard_map/ppermute | solution.py:49
  67.0 5.1 %collective-permute-start.5 = (bf16[8,1024]{1,0:T(8,128)(2,1)S(1)}, bf16[8,1024]{1,0:T(8,128)(2,1)S(1)}, u32[]{:S(2)}, u32[]{:S(2)}) collective-permute-start(bf16[8,1024]{1,0:T(8,128)(2,1)S(1)} %collective-permute-done.4), channel_id=1, source_target_pairs={{0,14},{2,0},{4,2},{6,4},{8,6},{10,8},{12,10},{14,12},{1,15},{3,1}... | collective-permute-start | bytes 49160 | tf_op jit(solution)/shard_map/ppermute | solution.py:49
  72.1 1.4 %collective-permute-done.5 = bf16[8,1024]{1,0:T(8,128)(2,1)S(1)} collective-permute-done((bf16[8,1024]{1,0:T(8,128)(2,1)S(1)}, bf16[8,1024]{1,0:T(8,128)(2,1)S(1)}, u32[]{:S(2)}, u32[]{:S(2)}) %collective-permute-start.5) | collective-permute-done | bytes 16416 | tf_op jit(solution)/shard_map/ppermute | solution.py:49
  73.5 5.0 %collective-permute-start.6 = (bf16[8,1024]{1,0:T(8,128)(2,1)S(1)}, bf16[8,1024]{1,0:T(8,128)(2,1)S(1)}, u32[]{:S(2)}, u32[]{:S(2)}) collective-permute-start(bf16[8,1024]{1,0:T(8,128)(2,1)S(1)} %collective-permute-done.5), channel_id=1, source_target_pairs={{0,14},{2,0},{4,2},{6,4},{8,6},{10,8},{12,10},{14,12},{1,15},{3,1}... | collective-permute-start | bytes 49160 | tf_op jit(solution)/shard_map/ppermute | solution.py:49
  78.5 1.4 %collective-permute-done.6 = bf16[8,1024]{1,0:T(8,128)(2,1)S(1)} collective-permute-done((bf16[8,1024]{1,0:T(8,128)(2,1)S(1)}, bf16[8,1024]{1,0:T(8,128)(2,1)S(1)}, u32[]{:S(2)}, u32[]{:S(2)}) %collective-permute-start.6) | collective-permute-done | bytes 16416 | tf_op jit(solution)/shard_map/ppermute | solution.py:49
  80.1 0.0 copy-done.1
  80.1 0.0 slice-start.1
  80.1 8.9 %fusion.2 = bf16[64,8192]{1,0:T(8,128)(2,1)S(1)} fusion(bf16[1024,8192]{1,0:T(8,128)(2,1)} %param.19, f32[8192]{0:T(1024)S(1)} %copy-done.1, bf16[128,1024]{1,0:T(8,128)(2,1)S(1)} %constant_dynamic-update-slice_fusion, s32[]{:T(128)S(6)} %select_n.18), kind=kOutput, calls=%fused_computation.3 | convolution fusion | flops 1075314688 | bytes 17989636 | tf_op jit(solution)/shard_map/dot_general | solution.py:55
  89.0 0.0 slice-done
  89.0 0.0 slice-done.1
  89.1 0.0 copy-start.5
  89.1 0.0 copy-start.2
  89.1 0.0 copy-start.3
  89.1 1.6 %convolution_bitcast_fusion.1 = f32[8,8,2,512]{3,1,0,2:T(8,128)S(1)} fusion(bf16[2,4096,512]{2,1,0:T(8,128)(2,1)S(1)} %bitcast.34, bf16[8,2,8,4096]{3,2,1,0:T(8,128)(2,1)S(1)} %bitcast.35), kind=kOutput, calls=%fused_computation.8 | convolution fusion | flops 536870912 | bytes 9699328 | tf_op jit(solution)/shard_map/rpw,pwo->rpo/dot_general | solution.py:59
  90.7 0.7 copy.20
  91.4 6.3 %all-to-all-start = ((f32[8,8,2,512]{3,1,2,0:T(8,128)}), f32[8,8,2,512]{3,1,2,0:T(8,128)S(1)}, u32[]{:S(2)}, u32[]{:S(2)}) async-start(f32[8,8,2,512]{3,1,2,0:T(8,128)} %copy.20), calls=%async_computation | async-start | bytes 524288 | tf_op jit(solution)/shard_map/all_to_all | solution.py:66
  97.6 0.0 reduce-scatter.2.cloned.1.call-start
  97.7 1.3 fusion.22
  99.0 0.1 broadcast_divide_fusion
  99.1 0.0 copy-done.5
  99.1 0.2 convolution_bitcast_fusion.2
  99.3 6.5 %all-to-all-done = f32[8,8,2,512]{3,1,2,0:T(8,128)S(1)} async-done(((f32[8,8,2,512]{3,1,2,0:T(8,128)}), f32[8,8,2,512]{3,1,2,0:T(8,128)S(1)}, u32[]{:S(2)}, u32[]{:S(2)}) %all-to-all-start) | async-done | bytes 262176 | tf_op jit(solution)/shard_map/all_to_all | solution.py:66
  105.9 0.0 copy-done.2
  105.9 0.2 convolution_convert_fusion
  106.1 5.6 %all_gather.7 = bf16[32,6,512]{2,0,1:T(8,128)(2,1)S(1)} all-gather(bf16[8,6,512]{2,0,1:T(8,128)(2,1)S(1)} %copy.23), channel_id=1, replica_groups=mesh['groups'=2,'expert'=4,'dp'=2,'tile'=2] {'dp','tile'}, dimensions={0}, use_global_device_ids=true | all-gather | bytes 245760 | tf_op jit(solution)/shard_map/all_gather | solution.py:77
  111.7 0.0 copy-done
  111.7 3.8 %convolution_bitcast_fusion = f32[32,6,512]{2,0,1:T(8,128)} fusion(bf16[6,512,512]{2,1,0:T(8,128)(2,1)S(1)} %copy-done, bf16[32,6,512]{2,0,1:T(8,128)(2,1)S(1)} %all_gather.7, bf16[6,512,512]{2,1,0:T(8,128)(2,1)} %param.24, f32[6,512]{1,0:T(8,128)S(1)} %copy-done.3), kind=kOutput, calls=%fused_computation.4 | convolution fusion | flops 201621504 | bytes 6893568 | tf_op jit(solution)/shard_map/rth,tho->rto/dot_general | solution.py:81
  115.5 0.0 reduce-scatter.2.cloned.1.call-update
  115.5 0.1 iota_compare_fusion.2
  115.6 19.2 %reduce-scatter.2.cloned.1.call-done = f32[8,6,512]{2,0,1:T(8,128)} async-done(((f32[32,6,512]{2,0,1:T(8,128)}), f32[8,6,512]{2,0,1:T(8,128)}) %reduce-scatter.2.cloned.1.call-update) | async-done | bytes 98320 | tf_op jit(solution)/shard_map/reduce_scatter | solution.py:80
  134.7 0.0 copy-done.4
  134.7 1.6 %select_convert_fusion = bf16[8,6,512]{2,0,1:T(8,128)(2,1)} fusion(f32[8,6,512]{2,0,1:T(8,128)} %reduce-scatter.2.cloned.1.call-done, f32[6,512]{1,0:T(8,128)S(1)} %copy-done.4, pred[8,6]{0,1:T(8,128)(4,1)S(1)} %iota_compare_fusion.2), kind=kLoop, calls=%fused_computation.25 | loop fusion | flops 73728 | bytes 159792 | tf_op jit(solution)/shard_map/convert_element_type | solution.py:89
  (24 shorter events, 0.1 us)
Async XLA Ops:
  6.5 105.2 %copy-start = (bf16[6,512,512]{2,1,0:T(8,128)(2,1)S(1)}, bf16[6,512,512]{2,1,0:T(8,128)(2,1)}, u32[]{:S(2)}) copy-start(bf16[6,512,512]{2,1,0:T(8,128)(2,1)} %param.26) | copy-start | bytes 9437188
  6.5 73.5 %copy-start.1 = (f32[8192]{0:T(1024)S(1)}, f32[8192]{0:T(1024)}, u32[]{:S(2)}) copy-start(f32[8192]{0:T(1024)} %param.20) | copy-start | bytes 98308
  6.5 27.9 %all-gather.2.cloned.1.call-start = ((), (), s32[]{:S(2)}) async-start(), calls=%async_computation.2 | async-start | bytes 2621440 | tf_op jit(solution)/shard_map/all_gather | solution.py:33
  36.4 4.8 %collective-permute-start = (bf16[8,1024]{1,0:T(8,128)(2,1)S(1)}, bf16[8,1024]{1,0:T(8,128)(2,1)S(1)}, u32[]{:S(2)}, u32[]{:S(2)}) collective-permute-start(bf16[8,1024]{1,0:T(8,128)(2,1)S(1)} %get-tuple-element.6), channel_id=1, source_target_pairs={{0,14},{2,0},{4,2},{6,4},{8,6},{10,8},{12,10},{14,12},{1,15},{3,1}... | collective-permute-start | bytes 49160 | tf_op jit(solution)/shard_map/ppermute | solution.py:49
  41.2 6.4 %collective-permute-start.1 = (bf16[8,1024]{1,0:T(8,128)(2,1)S(1)}, bf16[8,1024]{1,0:T(8,128)(2,1)S(1)}, u32[]{:S(2)}, u32[]{:S(2)}) collective-permute-start(bf16[8,1024]{1,0:T(8,128)(2,1)S(1)} %collective-permute-done), channel_id=1, source_target_pairs={{0,14},{2,0},{4,2},{6,4},{8,6},{10,8},{12,10},{14,12},{1,15},{3,1}... | collective-permute-start | bytes 49160 | tf_op jit(solution)/shard_map/ppermute | solution.py:49
  47.6 6.4 %collective-permute-start.2 = (bf16[8,1024]{1,0:T(8,128)(2,1)S(1)}, bf16[8,1024]{1,0:T(8,128)(2,1)S(1)}, u32[]{:S(2)}, u32[]{:S(2)}) collective-permute-start(bf16[8,1024]{1,0:T(8,128)(2,1)S(1)} %collective-permute-done.1), channel_id=1, source_target_pairs={{0,14},{2,0},{4,2},{6,4},{8,6},{10,8},{12,10},{14,12},{1,15},{3,1}... | collective-permute-start | bytes 49160 | tf_op jit(solution)/shard_map/ppermute | solution.py:49
  54.1 6.4 %collective-permute-start.3 = (bf16[8,1024]{1,0:T(8,128)(2,1)S(1)}, bf16[8,1024]{1,0:T(8,128)(2,1)S(1)}, u32[]{:S(2)}, u32[]{:S(2)}) collective-permute-start(bf16[8,1024]{1,0:T(8,128)(2,1)S(1)} %collective-permute-done.2), channel_id=1, source_target_pairs={{0,14},{2,0},{4,2},{6,4},{8,6},{10,8},{12,10},{14,12},{1,15},{3,1}... | collective-permute-start | bytes 49160 | tf_op jit(solution)/shard_map/ppermute | solution.py:49
  60.5 6.4 %collective-permute-start.4 = (bf16[8,1024]{1,0:T(8,128)(2,1)S(1)}, bf16[8,1024]{1,0:T(8,128)(2,1)S(1)}, u32[]{:S(2)}, u32[]{:S(2)}) collective-permute-start(bf16[8,1024]{1,0:T(8,128)(2,1)S(1)} %collective-permute-done.3), channel_id=1, source_target_pairs={{0,14},{2,0},{4,2},{6,4},{8,6},{10,8},{12,10},{14,12},{1,15},{3,1}... | collective-permute-start | bytes 49160 | tf_op jit(solution)/shard_map/ppermute | solution.py:49
  67.0 6.6 %collective-permute-start.5 = (bf16[8,1024]{1,0:T(8,128)(2,1)S(1)}, bf16[8,1024]{1,0:T(8,128)(2,1)S(1)}, u32[]{:S(2)}, u32[]{:S(2)}) collective-permute-start(bf16[8,1024]{1,0:T(8,128)(2,1)S(1)} %collective-permute-done.4), channel_id=1, source_target_pairs={{0,14},{2,0},{4,2},{6,4},{8,6},{10,8},{12,10},{14,12},{1,15},{3,1}... | collective-permute-start | bytes 49160 | tf_op jit(solution)/shard_map/ppermute | solution.py:49
  73.5 6.4 %collective-permute-start.6 = (bf16[8,1024]{1,0:T(8,128)(2,1)S(1)}, bf16[8,1024]{1,0:T(8,128)(2,1)S(1)}, u32[]{:S(2)}, u32[]{:S(2)}) collective-permute-start(bf16[8,1024]{1,0:T(8,128)(2,1)S(1)} %collective-permute-done.5), channel_id=1, source_target_pairs={{0,14},{2,0},{4,2},{6,4},{8,6},{10,8},{12,10},{14,12},{1,15},{3,1}... | collective-permute-start | bytes 49160 | tf_op jit(solution)/shard_map/ppermute | solution.py:49
  80.0 9.1 %slice-start = ((s8[8388608]{0:T(1024)(128)(4,1)}), s8[4194304]{0:T(1024)(128)(4,1)S(1)}, s32[]{:S(2)}) async-start(s8[8388608]{0:T(1024)(128)(4,1)} %bitcast.32), calls=%async_computation.4 | async-start | bytes 8388608
  80.1 9.0 %slice-start.1 = ((s8[8388608]{0:T(1024)(128)(4,1)}), s8[4194304]{0:T(1024)(128)(4,1)S(1)}, s32[]{:S(2)}) async-start(s8[8388608]{0:T(1024)(128)(4,1)} %bitcast.32), calls=%async_computation.5 | async-start | bytes 8388608
  89.1 10.1 %copy-start.5 = (s32[6,6]{1,0:T(8,128)S(1)}, s32[6,6]{1,0:T(8,128)}, u32[]{:S(2)}) copy-start(s32[6,6]{1,0:T(8,128)} %param.18) | copy-start | bytes 436
  89.1 16.8 %copy-start.2 = (f32[16,512]{1,0:T(8,128)S(1)}, f32[16,512]{1,0:T(8,128)}, u32[]{:S(2)}) copy-start(f32[16,512]{1,0:T(8,128)} %param.22) | copy-start | bytes 98308
  89.1 22.6 %copy-start.3 = (f32[6,512]{1,0:T(8,128)S(1)}, f32[6,512]{1,0:T(8,128)}, u32[]{:S(2)}) copy-start(f32[6,512]{1,0:T(8,128)} %param.25) | copy-start | bytes 36868
  91.4 14.5 %all-to-all-start = ((f32[8,8,2,512]{3,1,2,0:T(8,128)}), f32[8,8,2,512]{3,1,2,0:T(8,128)S(1)}, u32[]{:S(2)}, u32[]{:S(2)}) async-start(f32[8,8,2,512]{3,1,2,0:T(8,128)} %copy.20), calls=%async_computation | async-start | bytes 524288 | tf_op jit(solution)/shard_map/all_to_all | solution.py:66
  97.6 37.1 %reduce-scatter.2.cloned.1.call-start = ((), (), s32[]{:S(2)}) async-start(), calls=%async_computation.3 | async-start | bytes 491520 | tf_op jit(solution)/shard_map/reduce_scatter | solution.py:80
  111.7 3.8 %copy-start.6 = (s32[1,6]{1,0:T(1,128)S(1)}, s32[1,6]{1,0:T(1,128)}, u32[]{:S(2)}) copy-start(s32[1,6]{1,0:T(1,128)} %param.23) | copy-start | bytes 76
  111.7 23.0 %copy-start.4 = (f32[6,512]{1,0:T(8,128)S(1)}, f32[6,512]{1,0:T(8,128)}, u32[]{:S(2)}) copy-start(f32[6,512]{1,0:T(8,128)} %param.27) | copy-start | bytes 36868
Sparse Core Ops, SparseCore 0:
  8.9 25.5 all-gather.1
  115.6 19.0 reduce-scatter.1
